TPU v7x, 32 devices: a whole 2x2x4 slice. The times are simulated.
32 devices in a mesh: wrow: 16 (over z, y, x), kblk: 2 (over core).
Axes of the slice: x: 2, y: 2, z: 4, core: 2. Of those that a mesh axis runs over, the one named last changes fastest.
Arguments:
- conduction: bfloat16 [2, 4, 64, 16384], P('kblk', None, None, 'wrow'), may hold values from -6 to 6
- valence: bfloat16 [2, 4, 64, 16384], P(None, None, 'wrow', 'kblk'), may hold values from -6 to 6
- screened: bfloat16 [4, 16384, 16384], P(None, 'wrow', 'kblk'), may hold values from -0.00036621094 to 0.00036621094
- pair_block: int32 [2, 4], replicated, may hold values from 0 to 3, as said below
Outputs:
- kernel: float32 [2, 64, 256], P('kblk', 'wrow')
Inputs may be any that keep to these rules, and one draw needn't show every extreme that they name: `pair_block`: every one of the 4 blocks is selected by at least one pair and by at most 3 pairs; one block by exactly 3 pairs.
All inputs are finite; a program needn't handle non-finite values.
Results may differ from a plain program's by a relative error of at most 0.0029.
Values may be sent and summed in bfloat16 or wider, within the bound.
No kernel may reach another device: no remote copies, remote signals or barrier semaphores. Data moves between devices by JAX's collectives and lax.ppermute only.
A program may use at most 128 MiB of HBM per device.

v0:
```python
import jax
import jax.numpy as jnp
from jax import lax
from jax.sharding import PartitionSpec as P

C = 8
V = 8


def per_device(conduction, valence, screened, pair_block):
    gathered_cond = lax.all_gather(conduction, "kblk", axis=0, tiled=True)
    gathered_vale = lax.all_gather(valence, "wrow", axis=2, tiled=True)
    k_count = gathered_cond.shape[0]
    kp_count = gathered_cond.shape[1]
    pair_count = k_count * kp_count
    row_width = gathered_cond.shape[3]
    col_width = gathered_vale.shape[3]
    cond_flat = gathered_cond.reshape(pair_count, C * C, row_width)
    vale_flat = gathered_vale.reshape(pair_count, V * V, col_width)
    flat_blocks = pair_block.reshape(pair_count)
    pair_ids = jnp.arange(pair_count, dtype=jnp.int32)
    capacity = 3 * pair_count // 8
    block_count = screened.shape[0]

    def one_block(block, total):
        sort_keys = jnp.where(flat_blocks == block, 0, pair_count) + pair_ids
        chosen = jnp.argsort(sort_keys)[:capacity]
        present = (flat_blocks[chosen] == block).astype(jnp.float32)
        vale_sel = jnp.take(vale_flat, chosen, axis=0)
        cond_sel = jnp.take(cond_flat, chosen, axis=0)
        w_tile = lax.dynamic_index_in_dim(screened, block, 0, keepdims=False)
        screened_vale = jnp.einsum(
            "pvh,gh->pvg", vale_sel, w_tile, preferred_element_type=jnp.float32
        ).astype(jnp.bfloat16)
        tiles = jnp.einsum(
            "pcg,pvg->pcv", cond_sel, screened_vale, preferred_element_type=jnp.float32
        )
        placer = (pair_ids[:, None] == chosen[None, :]).astype(jnp.float32) * present[None, :]
        return total + jnp.einsum("sp,pcv->scv", placer, tiles, precision=lax.Precision.HIGHEST)

    terms = lax.fori_loop(
        0, block_count, one_block, jnp.zeros((pair_count, C * C, V * V), jnp.float32)
    )
    terms = terms.reshape(k_count, kp_count, C, C, V, V).transpose(0, 2, 4, 1, 3, 5)
    terms = terms.reshape(k_count, C * V, kp_count * C * V)
    by_block = lax.psum_scatter(terms, "kblk", scatter_dimension=0, tiled=True)
    return lax.psum_scatter(by_block, "wrow", scatter_dimension=1, tiled=True)


def solution(mesh):
    return jax.shard_map(
        per_device,
        mesh=mesh,
        in_specs=(
            P("kblk", None, None, "wrow"),
            P(None, None, "wrow", "kblk"),
            P(None, "wrow", "kblk"),
            P(),
        ),
        out_specs=P("kblk", "wrow", None),
        check_vma=False,
    )
```

profile of v0, /device:TPU:0, one launch (start us, length us, event | category | flops | bytes accessed | tf_op | source)
XLA Modules:
  0.0 346.6 jit_solution(13563379429917125649)
XLA Ops:
  6.5 2.2 copy.8
  10.4 114.8 %all-gather.5.cloned.1.call-done = bf16[2,4,64,8192]{3,1,0,2:T(4,128)(2,1)} async-done(((bf16[2,4,4,8192]{3,1,0,2:T(4,128)(2,1)}), bf16[2,4,64,8192]{3,1,0,2:T(4,128)(2,1)}) %all-gather.5.cloned.1.call-update) | async-done | bytes 8388624 | tf_op jit(solution)/shard_map/all_gather | solution.py:12
  125.2 11.2 %copy.11 = bf16[2,4,64,8192]{3,2,1,0:T(8,128)(2,1)} copy(bf16[2,4,64,8192]{3,1,0,2:T(4,128)(2,1)} %all-gather.5.cloned.1.call-done) | data formatting | bytes 16777216
  136.3 78.8 %while.15 = (s32[]{:T(128)}, f32[8,64,64]{2,0,1:T(8,128)S(1)}, s32[8]{0:T(128)S(1)}, bf16[8,64,1024]{2,1,0:T(8,128)(2,1)}, bf16[8,64,8192]{2,1,0:T(8,128)(2,1)},...) while((s32[]{:T(128)}, f32[8,64,64]{2,0,1:T(8,128)S(1)}, s32[8]{0:T(128)S(1)}, ...), condition=%wide.region_2.3_spmd.clone.clone, body=%wide.region_0.2_spmd.clone.clone.sunk | while | flops 3249603584 | bytes 28546016 | solution.py:41
  137.3 4.1 %gather_fusion = bf16[3,64,8192]{2,1,0:T(8,128)(2,1)S(1)} fusion(bf16[8,64,8192]{2,1,0:T(8,128)(2,1)} %get-tuple-element.260, s32[1024]{0:T(1024)S(1)} %pad_clamp_fusion.2), kind=kCustom, calls=%fused_computation.2.clone.clone.1 | custom fusion | bytes 6291468 | tf_op jit(solution)/shard_map/while/body/eval_jaxpr/jit(_take)/gather | solution.py:29
  141.5 10.3 %fusion.45 = bf16[3,64,1024]{2,1,0:T(8,128)(2,1)} fusion(bf16[4,1024,8192]{2,1,0:T(8,128)(2,1)} %get-tuple-element.261, s32[]{:T(128)} %get-tuple-element.248, bf16[3,64,8192]{2,1,0:T(8,128)(2,1)S(1)} %gather_fusion, pred[3]{0:T(512)(128)(4,1)S(1)} %get-tuple-element.239), kind=kOutput, calls=%fused_computation.10.clone.1 | convolution fusion | flops 3222994944 | bytes 20316676 | tf_op jit(solution)/shard_map/while/body/eval_jaxpr/pvh,gh->pvg/dot_general | solution.py:32
  151.8 1.8 gather_fusion.1
  153.6 1.3 fusion.46
  157.1 4.1 %gather_fusion = bf16[3,64,8192]{2,1,0:T(8,128)(2,1)S(1)} fusion(bf16[8,64,8192]{2,1,0:T(8,128)(2,1)} %get-tuple-element.260, s32[1024]{0:T(1024)S(1)} %pad_clamp_fusion.2), kind=kCustom, calls=%fused_computation.2.clone.clone.1 | custom fusion | bytes 6291468 | tf_op jit(solution)/shard_map/while/body/eval_jaxpr/jit(_take)/gather | solution.py:29
  161.2 10.3 %fusion.45 = bf16[3,64,1024]{2,1,0:T(8,128)(2,1)} fusion(bf16[4,1024,8192]{2,1,0:T(8,128)(2,1)} %get-tuple-element.261, s32[]{:T(128)} %get-tuple-element.248, bf16[3,64,8192]{2,1,0:T(8,128)(2,1)S(1)} %gather_fusion, pred[3]{0:T(512)(128)(4,1)S(1)} %get-tuple-element.239), kind=kOutput, calls=%fused_computation.10.clone.1 | convolution fusion | flops 3222994944 | bytes 20316676 | tf_op jit(solution)/shard_map/while/body/eval_jaxpr/pvh,gh->pvg/dot_general | solution.py:32
  171.5 1.8 gather_fusion.1
  173.3 1.3 fusion.46
  176.8 4.1 %gather_fusion = bf16[3,64,8192]{2,1,0:T(8,128)(2,1)S(1)} fusion(bf16[8,64,8192]{2,1,0:T(8,128)(2,1)} %get-tuple-element.260, s32[1024]{0:T(1024)S(1)} %pad_clamp_fusion.2), kind=kCustom, calls=%fused_computation.2.clone.clone.1 | custom fusion | bytes 6291468 | tf_op jit(solution)/shard_map/while/body/eval_jaxpr/jit(_take)/gather | solution.py:29
  180.9 10.3 %fusion.45 = bf16[3,64,1024]{2,1,0:T(8,128)(2,1)} fusion(bf16[4,1024,8192]{2,1,0:T(8,128)(2,1)} %get-tuple-element.261, s32[]{:T(128)} %get-tuple-element.248, bf16[3,64,8192]{2,1,0:T(8,128)(2,1)S(1)} %gather_fusion, pred[3]{0:T(512)(128)(4,1)S(1)} %get-tuple-element.239), kind=kOutput, calls=%fused_computation.10.clone.1 | convolution fusion | flops 3222994944 | bytes 20316676 | tf_op jit(solution)/shard_map/while/body/eval_jaxpr/pvh,gh->pvg/dot_general | solution.py:32
  191.2 1.8 gather_fusion.1
  193.0 1.3 fusion.46
  196.5 4.1 %gather_fusion = bf16[3,64,8192]{2,1,0:T(8,128)(2,1)S(1)} fusion(bf16[8,64,8192]{2,1,0:T(8,128)(2,1)} %get-tuple-element.260, s32[1024]{0:T(1024)S(1)} %pad_clamp_fusion.2), kind=kCustom, calls=%fused_computation.2.clone.clone.1 | custom fusion | bytes 6291468 | tf_op jit(solution)/shard_map/while/body/eval_jaxpr/jit(_take)/gather | solution.py:29
  200.6 10.3 %fusion.45 = bf16[3,64,1024]{2,1,0:T(8,128)(2,1)} fusion(bf16[4,1024,8192]{2,1,0:T(8,128)(2,1)} %get-tuple-element.261, s32[]{:T(128)} %get-tuple-element.248, bf16[3,64,8192]{2,1,0:T(8,128)(2,1)S(1)} %gather_fusion, pred[3]{0:T(512)(128)(4,1)S(1)} %get-tuple-element.239), kind=kOutput, calls=%fused_computation.10.clone.1 | convolution fusion | flops 3222994944 | bytes 20316676 | tf_op jit(solution)/shard_map/while/body/eval_jaxpr/pvh,gh->pvg/dot_general | solution.py:32
  210.9 1.8 gather_fusion.1
  212.7 1.3 fusion.46
  215.8 3.0 copy.17
  218.8 3.5 reshape.32
  222.3 6.4 %reduce-scatter.3.cloned.1.call-done = f32[1,64,256]{2,1,0:T(8,128)} async-done(((f32[2,64,256]{2,1,0:T(8,128)}), f32[1,64,256]{2,1,0:T(8,128)}) %reduce-scatter.3.cloned.1.call-update) | async-done | bytes 65552 | tf_op jit(solution)/shard_map/reduce_scatter | solution.py:46
  230.0 108.7 %all-reduce.3.cloned.1.call-done = f32[1,64,256]{2,1,0:T(8,128)} async-done(((f32[1,64,256]{2,1,0:T(8,128)}), f32[1,64,256]{2,1,0:T(8,128)}) %all-reduce.3.cloned.1.call-update) | async-done | bytes 65552
  (48 shorter events, 12.7 us)
Async XLA Ops:
  6.5 118.6 %all-gather.5.cloned.1.call-start = ((), (), s32[]{:S(2)}) async-start(), calls=%async_computation.2 | async-start | bytes 8912896 | tf_op jit(solution)/shard_map/all_gather | solution.py:12
  8.8 127.6 %all-gather.3.cloned.1.call-start = ((), (), s32[]{:S(2)}) async-start(), calls=%async_computation.1 | async-start | bytes 1572864 | tf_op jit(solution)/shard_map/all_gather | solution.py:11
  9.5 219.2 %reduce-scatter.3.cloned.1.call-start = ((), (), s32[]{:S(2)}) async-start(), calls=%async_computation.3 | async-start | bytes 196608 | tf_op jit(solution)/shard_map/reduce_scatter | solution.py:46
  215.8 13.0 %copy-start = (u32[32]{0:T(128)S(1)}, u32[32]{0:T(128)}, u32[]{:S(2)}) copy-start(u32[32]{0:T(128)} %constant.81) | copy-start | bytes 388
  222.2 116.5 %all-reduce.3.cloned.1.call-start = ((), (), s32[]{:S(2)}) async-start(), calls=%async_computation.4 | async-start | bytes 131072
Sparse Core Ops, SparseCore 0:
  10.1 115.0 all-gather.4
  126.7 7.1 all-gather.2
  222.4 6.3 reduce-scatter.2
  234.1 104.6 all-reduce.2
where the time goes:
time: 347 us
  waiting for transfers between devices  231 us (67%)
  local copies, waits for them, and re-layouts  49.3 us (14%)
  matrix products  48.4 us (14%)
  between operations  13.8 us (4%)
  other arithmetic  3.96 us (1%)
    all_gather x1, waiting for transfers between devices, per_device(): gathered_vale = lax.all_gather(valence, 'wrow', axis=2, tiled=True)  115 us
    unnamed x5, waiting for transfers between devices  109 us
    dot_general x4, matrix products, one_block(): jnp.einsum('pvh,gh->pvg', vale_sel, w_tile, preferred_element_type=jnp.fl...  41.1 us
    gather x4, local copies, waits for them, and re-layouts, one_block(): vale_sel = jnp.take(vale_flat, chosen, axis=0)  16.5 us
    unnamed x6, local copies, waits for them, and re-layouts  15.3 us
    gather x4, local copies, waits for them, and re-layouts, one_block(): cond_sel = jnp.take(cond_flat, chosen, axis=0)  7.18 us
  transfers between devices with their start and end apart: 4, of which 3 were waited for; matrix products, arithmetic and copies ran while one was open for 4% of the time, Pallas kernels for 0%

commit v1 on v0

--- a/solution.py
+++ b/solution.py
@@ -9,7 +9,12 @@
 
 def per_device(conduction, valence, screened, pair_block):
     gathered_cond = lax.all_gather(conduction, "kblk", axis=0, tiled=True)
-    gathered_vale = lax.all_gather(valence, "wrow", axis=2, tiled=True)
+    ring = [valence]
+    for hop in range(15):
+        ring.append(lax.ppermute(ring[-1], "wrow", [(dev, (dev + 1) % 16) for dev in range(16)]))
+    gathered_vale = jnp.roll(
+        jnp.concatenate(ring[::-1], axis=2), (lax.axis_index("wrow") + 1) * ring[0].shape[2], axis=2
+    )
     k_count = gathered_cond.shape[0]
     kp_count = gathered_cond.shape[1]
     pair_count = k_count * kp_count

time: 347 us -> 541 us (1.56)
  waiting for transfers between devices: 231 us -> 340 us
  local copies, waits for them, and re-layouts: 49.3 us -> 127 us
    ppermute x0 -> x15, waiting for transfers between devices: none -> 228 us  [per_device(): lax.ppermute(ring[-1], 'wrow', [(dev, (dev + 1) % 16) for dev in range(16)])]
    all_gather x1 -> x0, waiting for transfers between devices: 115 us -> none  [per_device(): gathered_vale = lax.all_gather(valence, 'wrow', axis=2, tiled=True)]
    concatenate x0 -> x1, local copies, waits for them, and re-layouts: none -> 76.5 us  [per_device(): jnp.roll(jnp.concatenate(ring[::-1], axis=2), (lax.axis_index('wrow') + 1...]
    dynamic_slice x0 -> x1, local copies, waits for them, and re-layouts: none -> 9.27 us  [per_device(): jnp.roll(jnp.concatenate(ring[::-1], axis=2), (lax.axis_index('wrow') + 1...]
    unnamed x6 -> x18, local copies, waits for them, and re-layouts: 15.3 us -> 7.49 us
    unnamed x5 -> x4, waiting for transfers between devices: 109 us -> 109 us
  transfers between devices with their start and end apart: 4 -> 18, of which waited for: 3 -> 17; matrix products, arithmetic and copies ran while one was open for 4% -> 16% of each run, Pallas kernels for 0% -> 0%
where the time goes in v1:
time: 541 us; the launch traced here: 536 us
  waiting for transfers between devices  340 us (63%)
  local copies, waits for them, and re-layouts  127 us (23%)
  matrix products  48.2 us (9%)
  between operations  13.9 us (3%)
    ppermute x15, waiting for transfers between devices, per_device(): lax.ppermute(ring[-1], 'wrow', [(dev, (dev + 1) % 16) for dev in range(16)])  228 us
    unnamed x4, waiting for transfers between devices  109 us
    concatenate x1, local copies, waits for them, and re-layouts, per_device(): jnp.roll(jnp.concatenate(ring[::-1], axis=2), (lax.axis_index('wrow') + 1...  76.5 us
    dot_general x4, matrix products, one_block(): jnp.einsum('pvh,gh->pvg', vale_sel, w_tile, preferred_element_type=jnp.fl...  40.9 us
    gather x4, local copies, waits for them, and re-layouts, one_block(): vale_sel = jnp.take(vale_flat, chosen, axis=0)  16.5 us
  transfers between devices with their start and end apart: 18, of which 17 were waited for; matrix products, arithmetic and copies ran while one was open for 16% of the time, Pallas kernels for 0%

profile of v1, /device:TPU:0, one launch (start us, length us, event | category | flops | bytes accessed | tf_op | source)
XLA Modules:
  0.0 536.5 jit_solution(8452592247526096201)
XLA Ops:
  9.5 16.1 %collective-permute-done = bf16[2,4,4,8192]{3,2,1,0:T(4,128)(2,1)S(1)} collective-permute-done((bf16[2,4,4,8192]{3,2,1,0:T(4,128)(2,1)}, bf16[2,4,4,8192]{3,2,1,0:T(4,128)(2,1)S(1)}, u32[]{:S(2)}, u32[]{:S(2)}) %collective-permute-start) | collective-permute-done | bytes 524320 | tf_op jit(solution)/shard_map/ppermute | solution.py:14
  25.6 16.7 %collective-permute-done.1 = bf16[2,4,4,8192]{3,2,1,0:T(4,128)(2,1)S(1)} collective-permute-done((bf16[2,4,4,8192]{3,2,1,0:T(4,128)(2,1)S(1)}, bf16[2,4,4,8192]{3,2,1,0:T(4,128)(2,1)S(1)}, u32[]{:S(2)}, u32[]{:S(2)}) %collective-permute-start.1) | collective-permute-done | bytes 524320 | tf_op jit(solution)/shard_map/ppermute | solution.py:14
  42.3 15.8 %collective-permute-done.2 = bf16[2,4,4,8192]{3,2,1,0:T(4,128)(2,1)S(1)} collective-permute-done((bf16[2,4,4,8192]{3,2,1,0:T(4,128)(2,1)S(1)}, bf16[2,4,4,8192]{3,2,1,0:T(4,128)(2,1)S(1)}, u32[]{:S(2)}, u32[]{:S(2)}) %collective-permute-start.2) | collective-permute-done | bytes 524320 | tf_op jit(solution)/shard_map/ppermute | solution.py:14
  58.1 15.0 %collective-permute-done.3 = bf16[2,4,4,8192]{3,2,1,0:T(4,128)(2,1)S(1)} collective-permute-done((bf16[2,4,4,8192]{3,2,1,0:T(4,128)(2,1)S(1)}, bf16[2,4,4,8192]{3,2,1,0:T(4,128)(2,1)S(1)}, u32[]{:S(2)}, u32[]{:S(2)}) %collective-permute-start.3) | collective-permute-done | bytes 524320 | tf_op jit(solution)/shard_map/ppermute | solution.py:14
  73.1 14.1 %collective-permute-done.4 = bf16[2,4,4,8192]{3,2,1,0:T(4,128)(2,1)S(1)} collective-permute-done((bf16[2,4,4,8192]{3,2,1,0:T(4,128)(2,1)S(1)}, bf16[2,4,4,8192]{3,2,1,0:T(4,128)(2,1)S(1)}, u32[]{:S(2)}, u32[]{:S(2)}) %collective-permute-start.4) | collective-permute-done | bytes 524320 | tf_op jit(solution)/shard_map/ppermute | solution.py:14
  87.2 13.3 %collective-permute-done.5 = bf16[2,4,4,8192]{3,2,1,0:T(4,128)(2,1)S(1)} collective-permute-done((bf16[2,4,4,8192]{3,2,1,0:T(4,128)(2,1)S(1)}, bf16[2,4,4,8192]{3,2,1,0:T(4,128)(2,1)S(1)}, u32[]{:S(2)}, u32[]{:S(2)}) %collective-permute-start.5) | collective-permute-done | bytes 524320 | tf_op jit(solution)/shard_map/ppermute | solution.py:14
  100.5 12.8 %collective-permute-done.6 = bf16[2,4,4,8192]{3,2,1,0:T(4,128)(2,1)S(1)} collective-permute-done((bf16[2,4,4,8192]{3,2,1,0:T(4,128)(2,1)S(1)}, bf16[2,4,4,8192]{3,2,1,0:T(4,128)(2,1)S(1)}, u32[]{:S(2)}, u32[]{:S(2)}) %collective-permute-start.6) | collective-permute-done | bytes 524320 | tf_op jit(solution)/shard_map/ppermute | solution.py:14
  114.1 13.1 %collective-permute-done.7 = bf16[2,4,4,8192]{3,2,1,0:T(4,128)(2,1)S(1)} collective-permute-done((bf16[2,4,4,8192]{3,2,1,0:T(4,128)(2,1)S(1)}, bf16[2,4,4,8192]{3,2,1,0:T(4,128)(2,1)S(1)}, u32[]{:S(2)}, u32[]{:S(2)}) %collective-permute-start.7) | collective-permute-done | bytes 524320 | tf_op jit(solution)/shard_map/ppermute | solution.py:14
  128.0 14.3 %collective-permute-done.8 = bf16[2,4,4,8192]{3,2,1,0:T(4,128)(2,1)S(1)} collective-permute-done((bf16[2,4,4,8192]{3,2,1,0:T(4,128)(2,1)S(1)}, bf16[2,4,4,8192]{3,2,1,0:T(4,128)(2,1)S(1)}, u32[]{:S(2)}, u32[]{:S(2)}) %collective-permute-start.8) | collective-permute-done | bytes 524320 | tf_op jit(solution)/shard_map/ppermute | solution.py:14
  143.0 15.4 %collective-permute-done.9 = bf16[2,4,4,8192]{3,2,1,0:T(4,128)(2,1)S(1)} collective-permute-done((bf16[2,4,4,8192]{3,2,1,0:T(4,128)(2,1)S(1)}, bf16[2,4,4,8192]{3,2,1,0:T(4,128)(2,1)S(1)}, u32[]{:S(2)}, u32[]{:S(2)}) %collective-permute-start.9) | collective-permute-done | bytes 524320 | tf_op jit(solution)/shard_map/ppermute | solution.py:14
  159.2 16.5 %collective-permute-done.10 = bf16[2,4,4,8192]{3,2,1,0:T(4,128)(2,1)S(1)} collective-permute-done((bf16[2,4,4,8192]{3,2,1,0:T(4,128)(2,1)S(1)}, bf16[2,4,4,8192]{3,2,1,0:T(4,128)(2,1)S(1)}, u32[]{:S(2)}, u32[]{:S(2)}) %collective-permute-start.10) | collective-permute-done | bytes 524320 | tf_op jit(solution)/shard_map/ppermute | solution.py:14
  176.6 17.7 %collective-permute-done.11 = bf16[2,4,4,8192]{3,2,1,0:T(4,128)(2,1)S(1)} collective-permute-done((bf16[2,4,4,8192]{3,2,1,0:T(4,128)(2,1)S(1)}, bf16[2,4,4,8192]{3,2,1,0:T(4,128)(2,1)S(1)}, u32[]{:S(2)}, u32[]{:S(2)}) %collective-permute-start.11) | collective-permute-done | bytes 524320 | tf_op jit(solution)/shard_map/ppermute | solution.py:14
  195.1 18.0 %collective-permute-done.12 = bf16[2,4,4,8192]{3,2,1,0:T(4,128)(2,1)S(1)} collective-permute-done((bf16[2,4,4,8192]{3,2,1,0:T(4,128)(2,1)S(1)}, bf16[2,4,4,8192]{3,2,1,0:T(4,128)(2,1)S(1)}, u32[]{:S(2)}, u32[]{:S(2)}) %collective-permute-start.12) | collective-permute-done | bytes 524320 | tf_op jit(solution)/shard_map/ppermute | solution.py:14
  213.9 16.6 %collective-permute-done.13 = bf16[2,4,4,8192]{3,2,1,0:T(4,128)(2,1)} collective-permute-done((bf16[2,4,4,8192]{3,2,1,0:T(4,128)(2,1)S(1)}, bf16[2,4,4,8192]{3,2,1,0:T(4,128)(2,1)}, u32[]{:S(2)}, u32[]{:S(2)}) %collective-permute-start.13) | collective-permute-done | bytes 524320 | tf_op jit(solution)/shard_map/ppermute | solution.py:14
  231.3 12.2 %collective-permute-done.14 = bf16[2,4,4,8192]{3,2,1,0:T(4,128)(2,1)} collective-permute-done((bf16[2,4,4,8192]{3,2,1,0:T(4,128)(2,1)}, bf16[2,4,4,8192]{3,2,1,0:T(4,128)(2,1)}, u32[]{:S(2)}, u32[]{:S(2)}) %collective-permute-start.14) | collective-permute-done | bytes 524320 | tf_op jit(solution)/shard_map/ppermute | solution.py:14
  243.6 76.5 %concatenate.6 = bf16[2,4,128,8192]{3,2,1,0:T(8,128)(2,1)} concatenate(bf16[2,4,4,8192]{3,2,1,0:T(4,128)(2,1)} %collective-permute-done.14, bf16[2,4,4,8192]{3,2,1,0:T(4,128)(2,1)} %collective-permute-done.13, bf16[2,4,4,8192]{3,2,1,0:T(4,128)(2,1)} %copy-done.6, bf16[2,4,4,8192]{3,2,1,0:T(4,128)(2,1)} %copy-done.5, bf16[2,4,4,8192]{3,2,1,0:T(4,128)(2,1)} %copy-done.4, ...), dimensions={2} | concatenate | bytes 33554432 | tf_op jit(solution)/shard_map/jit(_roll_dynamic)/concatenate | solution.py:15
  320.0 9.3 %constant_dynamic-slice_fusion.1 = bf16[2,4,64,8192]{3,2,1,0:T(8,128)(2,1)} fusion(bf16[2,4,128,8192]{3,2,1,0:T(8,128)(2,1)} %concatenate.6, s32[]{:T(128)S(6)} %select_n.56), kind=kLoop, calls=%fused_computation.35 | loop fusion | bytes 16777220 | tf_op jit(solution)/shard_map/jit(_roll_dynamic)/dynamic_slice | solution.py:15
  329.3 78.6 %while.15 = (s32[]{:T(128)}, f32[8,64,64]{2,0,1:T(8,128)S(1)}, s32[8]{0:T(128)S(1)}, bf16[8,64,1024]{2,1,0:T(8,128)(2,1)}, bf16[8,64,8192]{2,1,0:T(8,128)(2,1)},...) while((s32[]{:T(128)}, f32[8,64,64]{2,0,1:T(8,128)S(1)}, s32[8]{0:T(128)S(1)}, ...), condition=%wide.region_2.3_spmd.clone.clone, body=%wide.region_0.2_spmd.clone.clone.sunk | while | flops 3249603584 | bytes 28546016 | solution.py:46
  330.3 4.1 gather_fusion
  334.4 10.2 %fusion.45 = bf16[3,64,1024]{2,1,0:T(8,128)(2,1)} fusion(bf16[4,1024,8192]{2,1,0:T(8,128)(2,1)} %get-tuple-element.255, s32[]{:T(128)} %get-tuple-element.242, bf16[3,64,8192]{2,1,0:T(8,128)(2,1)S(1)} %gather_fusion, pred[3]{0:T(512)(128)(4,1)S(1)} %get-tuple-element.233), kind=kOutput, calls=%fused_computation.10.clone.1 | convolution fusion | flops 3222994944 | bytes 20316676 | tf_op jit(solution)/shard_map/while/body/eval_jaxpr/pvh,gh->pvg/dot_general | solution.py:37
  354.1 10.2 %fusion.45 = bf16[3,64,1024]{2,1,0:T(8,128)(2,1)} fusion(bf16[4,1024,8192]{2,1,0:T(8,128)(2,1)} %get-tuple-element.255, s32[]{:T(128)} %get-tuple-element.242, bf16[3,64,8192]{2,1,0:T(8,128)(2,1)S(1)} %gather_fusion, pred[3]{0:T(512)(128)(4,1)S(1)} %get-tuple-element.233), kind=kOutput, calls=%fused_computation.10.clone.1 | convolution fusion | flops 3222994944 | bytes 20316676 | tf_op jit(solution)/shard_map/while/body/eval_jaxpr/pvh,gh->pvg/dot_general | solution.py:37
  373.7 10.2 %fusion.45 = bf16[3,64,1024]{2,1,0:T(8,128)(2,1)} fusion(bf16[4,1024,8192]{2,1,0:T(8,128)(2,1)} %get-tuple-element.255, s32[]{:T(128)} %get-tuple-element.242, bf16[3,64,8192]{2,1,0:T(8,128)(2,1)S(1)} %gather_fusion, pred[3]{0:T(512)(128)(4,1)S(1)} %get-tuple-element.233), kind=kOutput, calls=%fused_computation.10.clone.1 | convolution fusion | flops 3222994944 | bytes 20316676 | tf_op jit(solution)/shard_map/while/body/eval_jaxpr/pvh,gh->pvg/dot_general | solution.py:37
  393.4 10.2 %fusion.45 = bf16[3,64,1024]{2,1,0:T(8,128)(2,1)} fusion(bf16[4,1024,8192]{2,1,0:T(8,128)(2,1)} %get-tuple-element.255, s32[]{:T(128)} %get-tuple-element.242, bf16[3,64,8192]{2,1,0:T(8,128)(2,1)S(1)} %gather_fusion, pred[3]{0:T(512)(128)(4,1)S(1)} %get-tuple-element.233), kind=kOutput, calls=%fused_computation.10.clone.1 | convolution fusion | flops 3222994944 | bytes 20316676 | tf_op jit(solution)/shard_map/while/body/eval_jaxpr/pvh,gh->pvg/dot_general | solution.py:37
  419.8 108.8 %all-reduce.3.cloned.1.call-done = f32[1,64,256]{2,1,0:T(8,128)} async-done(((f32[1,64,256]{2,1,0:T(8,128)}), f32[1,64,256]{2,1,0:T(8,128)}) %all-reduce.3.cloned.1.call-update) | async-done | bytes 65552
  (89 shorter events, 55.3 us)
Async XLA Ops:
  6.5 322.7 %all-gather.2.cloned.1.call-start = ((), (), s32[]{:S(2)}) async-start(), calls=%async_computation.1 | async-start | bytes 1572864 | tf_op jit(solution)/shard_map/all_gather | solution.py:11
  6.5 19.1 %collective-permute-start = (bf16[2,4,4,8192]{3,2,1,0:T(4,128)(2,1)}, bf16[2,4,4,8192]{3,2,1,0:T(4,128)(2,1)S(1)}, u32[]{:S(2)}, u32[]{:S(2)}) collective-permute-start(bf16[2,4,4,8192]{3,2,1,0:T(4,128)(2,1)} %param.7), channel_id=1, source_target_pairs={{0,2},{2,4},{4,6},{6,8},{8,10},{10,12},{12,14},{14,16},{16,18},{18... | collective-permute-start | bytes 1572872 | tf_op jit(solution)/shard_map/ppermute | solution.py:14
  25.6 16.7 %collective-permute-start.1 = (bf16[2,4,4,8192]{3,2,1,0:T(4,128)(2,1)S(1)}, bf16[2,4,4,8192]{3,2,1,0:T(4,128)(2,1)S(1)}, u32[]{:S(2)}, u32[]{:S(2)}) collective-permute-start(bf16[2,4,4,8192]{3,2,1,0:T(4,128)(2,1)S(1)} %collective-permute-done), channel_id=1, source_target_pairs={{0,2},{2,4},{4,6},{6,8},{8,10},{10,12},{12,14},{14,16},{16,18},{18... | collective-permute-start | bytes 1572872 | tf_op jit(solution)/shard_map/ppermute | solution.py:14
  42.3 15.8 %collective-permute-start.2 = (bf16[2,4,4,8192]{3,2,1,0:T(4,128)(2,1)S(1)}, bf16[2,4,4,8192]{3,2,1,0:T(4,128)(2,1)S(1)}, u32[]{:S(2)}, u32[]{:S(2)}) collective-permute-start(bf16[2,4,4,8192]{3,2,1,0:T(4,128)(2,1)S(1)} %collective-permute-done.1), channel_id=1, source_target_pairs={{0,2},{2,4},{4,6},{6,8},{8,10},{10,12},{12,14},{14,16},{16,18},{18... | collective-permute-start | bytes 1572872 | tf_op jit(solution)/shard_map/ppermute | solution.py:14
  58.1 15.0 %collective-permute-start.3 = (bf16[2,4,4,8192]{3,2,1,0:T(4,128)(2,1)S(1)}, bf16[2,4,4,8192]{3,2,1,0:T(4,128)(2,1)S(1)}, u32[]{:S(2)}, u32[]{:S(2)}) collective-permute-start(bf16[2,4,4,8192]{3,2,1,0:T(4,128)(2,1)S(1)} %collective-permute-done.2), channel_id=1, source_target_pairs={{0,2},{2,4},{4,6},{6,8},{8,10},{10,12},{12,14},{14,16},{16,18},{18... | collective-permute-start | bytes 1572872 | tf_op jit(solution)/shard_map/ppermute | solution.py:14
  73.1 14.1 %collective-permute-start.4 = (bf16[2,4,4,8192]{3,2,1,0:T(4,128)(2,1)S(1)}, bf16[2,4,4,8192]{3,2,1,0:T(4,128)(2,1)S(1)}, u32[]{:S(2)}, u32[]{:S(2)}) collective-permute-start(bf16[2,4,4,8192]{3,2,1,0:T(4,128)(2,1)S(1)} %collective-permute-done.3), channel_id=1, source_target_pairs={{0,2},{2,4},{4,6},{6,8},{8,10},{10,12},{12,14},{14,16},{16,18},{18... | collective-permute-start | bytes 1572872 | tf_op jit(solution)/shard_map/ppermute | solution.py:14
  87.2 13.3 %collective-permute-start.5 = (bf16[2,4,4,8192]{3,2,1,0:T(4,128)(2,1)S(1)}, bf16[2,4,4,8192]{3,2,1,0:T(4,128)(2,1)S(1)}, u32[]{:S(2)}, u32[]{:S(2)}) collective-permute-start(bf16[2,4,4,8192]{3,2,1,0:T(4,128)(2,1)S(1)} %collective-permute-done.4), channel_id=1, source_target_pairs={{0,2},{2,4},{4,6},{6,8},{8,10},{10,12},{12,14},{14,16},{16,18},{18... | collective-permute-start | bytes 1572872 | tf_op jit(solution)/shard_map/ppermute | solution.py:14
  100.5 12.8 %collective-permute-start.6 = (bf16[2,4,4,8192]{3,2,1,0:T(4,128)(2,1)S(1)}, bf16[2,4,4,8192]{3,2,1,0:T(4,128)(2,1)S(1)}, u32[]{:S(2)}, u32[]{:S(2)}) collective-permute-start(bf16[2,4,4,8192]{3,2,1,0:T(4,128)(2,1)S(1)} %collective-permute-done.5), channel_id=1, source_target_pairs={{0,2},{2,4},{4,6},{6,8},{8,10},{10,12},{12,14},{14,16},{16,18},{18... | collective-permute-start | bytes 1572872 | tf_op jit(solution)/shard_map/ppermute | solution.py:14
  113.3 0.8 copy-start
  114.1 13.1 %collective-permute-start.7 = (bf16[2,4,4,8192]{3,2,1,0:T(4,128)(2,1)S(1)}, bf16[2,4,4,8192]{3,2,1,0:T(4,128)(2,1)S(1)}, u32[]{:S(2)}, u32[]{:S(2)}) collective-permute-start(bf16[2,4,4,8192]{3,2,1,0:T(4,128)(2,1)S(1)} %collective-permute-done.6), channel_id=1, source_target_pairs={{0,2},{2,4},{4,6},{6,8},{8,10},{10,12},{12,14},{14,16},{16,18},{18... | collective-permute-start | bytes 1572872 | tf_op jit(solution)/shard_map/ppermute | solution.py:14
  128.0 14.3 %collective-permute-start.8 = (bf16[2,4,4,8192]{3,2,1,0:T(4,128)(2,1)S(1)}, bf16[2,4,4,8192]{3,2,1,0:T(4,128)(2,1)S(1)}, u32[]{:S(2)}, u32[]{:S(2)}) collective-permute-start(bf16[2,4,4,8192]{3,2,1,0:T(4,128)(2,1)S(1)} %collective-permute-done.7), channel_id=1, source_target_pairs={{0,2},{2,4},{4,6},{6,8},{8,10},{10,12},{12,14},{14,16},{16,18},{18... | collective-permute-start | bytes 1572872 | tf_op jit(solution)/shard_map/ppermute | solution.py:14
  142.2 0.8 copy-start.2
  143.0 15.4 %collective-permute-start.9 = (bf16[2,4,4,8192]{3,2,1,0:T(4,128)(2,1)S(1)}, bf16[2,4,4,8192]{3,2,1,0:T(4,128)(2,1)S(1)}, u32[]{:S(2)}, u32[]{:S(2)}) collective-permute-start(bf16[2,4,4,8192]{3,2,1,0:T(4,128)(2,1)S(1)} %collective-permute-done.8), channel_id=1, source_target_pairs={{0,2},{2,4},{4,6},{6,8},{8,10},{10,12},{12,14},{14,16},{16,18},{18... | collective-permute-start | bytes 1572872 | tf_op jit(solution)/shard_map/ppermute | solution.py:14
  159.2 16.5 %collective-permute-start.10 = (bf16[2,4,4,8192]{3,2,1,0:T(4,128)(2,1)S(1)}, bf16[2,4,4,8192]{3,2,1,0:T(4,128)(2,1)S(1)}, u32[]{:S(2)}, u32[]{:S(2)}) collective-permute-start(bf16[2,4,4,8192]{3,2,1,0:T(4,128)(2,1)S(1)} %collective-permute-done.9), channel_id=1, source_target_pairs={{0,2},{2,4},{4,6},{6,8},{8,10},{10,12},{12,14},{14,16},{16,18},{18... | collective-permute-start | bytes 1572872 | tf_op jit(solution)/shard_map/ppermute | solution.py:14
  175.8 0.8 copy-start.4
  176.6 17.7 %collective-permute-start.11 = (bf16[2,4,4,8192]{3,2,1,0:T(4,128)(2,1)S(1)}, bf16[2,4,4,8192]{3,2,1,0:T(4,128)(2,1)S(1)}, u32[]{:S(2)}, u32[]{:S(2)}) collective-permute-start(bf16[2,4,4,8192]{3,2,1,0:T(4,128)(2,1)S(1)} %collective-permute-done.10), channel_id=1, source_target_pairs={{0,2},{2,4},{4,6},{6,8},{8,10},{10,12},{12,14},{14,16},{16,18},{18... | collective-permute-start | bytes 1572872 | tf_op jit(solution)/shard_map/ppermute | solution.py:14
  194.3 0.8 copy-start.5
  195.1 18.0 %collective-permute-start.12 = (bf16[2,4,4,8192]{3,2,1,0:T(4,128)(2,1)S(1)}, bf16[2,4,4,8192]{3,2,1,0:T(4,128)(2,1)S(1)}, u32[]{:S(2)}, u32[]{:S(2)}) collective-permute-start(bf16[2,4,4,8192]{3,2,1,0:T(4,128)(2,1)S(1)} %collective-permute-done.11), channel_id=1, source_target_pairs={{0,2},{2,4},{4,6},{6,8},{8,10},{10,12},{12,14},{14,16},{16,18},{18... | collective-permute-start | bytes 1572872 | tf_op jit(solution)/shard_map/ppermute | solution.py:14
  213.0 0.8 copy-start.6
  213.9 16.6 %collective-permute-start.13 = (bf16[2,4,4,8192]{3,2,1,0:T(4,128)(2,1)S(1)}, bf16[2,4,4,8192]{3,2,1,0:T(4,128)(2,1)}, u32[]{:S(2)}, u32[]{:S(2)}) collective-permute-start(bf16[2,4,4,8192]{3,2,1,0:T(4,128)(2,1)S(1)} %collective-permute-done.12), channel_id=1, source_target_pairs={{0,2},{2,4},{4,6},{6,8},{8,10},{10,12},{12,14},{14,16},{16,18},{18... | collective-permute-start | bytes 1572872 | tf_op jit(solution)/shard_map/ppermute | solution.py:14
  230.5 13.1 %collective-permute-start.14 = (bf16[2,4,4,8192]{3,2,1,0:T(4,128)(2,1)}, bf16[2,4,4,8192]{3,2,1,0:T(4,128)(2,1)}, u32[]{:S(2)}, u32[]{:S(2)}) collective-permute-start(bf16[2,4,4,8192]{3,2,1,0:T(4,128)(2,1)} %collective-permute-done.13), channel_id=1, source_target_pairs={{0,2},{2,4},{4,6},{6,8},{8,10},{10,12},{12,14},{14,16},{16,18},{18... | collective-permute-start | bytes 1572872 | tf_op jit(solution)/shard_map/ppermute | solution.py:14
  230.5 188.0 %reduce-scatter.3.cloned.1.call-start = ((), (), s32[]{:S(2)}) async-start(), calls=%async_computation.2 | async-start | bytes 196608 | tf_op jit(solution)/shard_map/reduce_scatter | solution.py:51
  408.5 10.1 %copy-start.7 = (u32[32]{0:T(128)S(1)}, u32[32]{0:T(128)}, u32[]{:S(2)}) copy-start(u32[32]{0:T(128)} %constant.112) | copy-start | bytes 388
  414.9 113.7 %all-reduce.3.cloned.1.call-start = ((), (), s32[]{:S(2)}) async-start(), calls=%async_computation.3 | async-start | bytes 131072
  (2 other events, 1.6 us)
Sparse Core Ops, SparseCore 0:
  230.6 10.3 all-gather.1
  415.0 3.4 reduce-scatter.2
  424.0 104.5 all-reduce.2
